TPU v7x, 32 devices: a whole 2x2x4 slice. The times are simulated.
32 devices in a mesh: dp: 8 (over z, core), fsdp: 4 (over y, x).
Axes of the slice: x: 2, y: 2, z: 4, core: 2. Of those that a mesh axis runs over, the one named last changes fastest.
Arguments:
- tokens: bfloat16 [32, 1024, 768], P(('dp', 'fsdp')), may hold values from -6 to 6
- lengths: int32 [32], P(('dp', 'fsdp')), may hold values from 1 to 1024, as said below
- keep_attn: int32 [32, 1024, 768], P(('dp', 'fsdp')), may hold values 0 or 1
- keep_ffn: int32 [32, 1024, 768], P(('dp', 'fsdp')), may hold values 0 or 1
- partners: int32 [32], replicated, may hold values from 0 to 31, as said below
- out_cot: bfloat16 [32, 1024, 768], P(('dp', 'fsdp')), may hold values from -6 to 6
- w_qkv: bfloat16 [768, 2304], P(('dp', 'fsdp')), may hold values from -0.21875 to 0.21875
- b_qv: bfloat16 [1536], P(('dp', 'fsdp')), may hold values from -3 to 3
- w_out: bfloat16 [768, 768], P(('dp', 'fsdp')), may hold values from -6 to 6
- b_out: bfloat16 [768], P(('dp', 'fsdp')), may hold values from -3 to 3
- ln1_gain: bfloat16 [768], P(('dp', 'fsdp')), may hold values from 0.099609375 to 1.8984375
- ln1_bias: bfloat16 [768], P(('dp', 'fsdp')), may hold values from -3 to 3
- w_up: bfloat16 [768, 3072], P(('dp', 'fsdp')), may hold values from -0.21875 to 0.21875
- b_up: bfloat16 [3072], P(('dp', 'fsdp')), may hold values from -3 to 3
- w_down: bfloat16 [3072, 768], P(('dp', 'fsdp')), may hold values from -0.109375 to 0.109375
- b_down: bfloat16 [768], P(('dp', 'fsdp')), may hold values from -3 to 3
- ln2_gain: bfloat16 [768], P(('dp', 'fsdp')), may hold values from 0.099609375 to 1.8984375
- ln2_bias: bfloat16 [768], P(('dp', 'fsdp')), may hold values from -3 to 3
- w_pool: bfloat16 [768, 768], P(('dp', 'fsdp')), may hold values from -0.21875 to 0.21875
- b_pool: bfloat16 [768], P(('dp', 'fsdp')), may hold values from -3 to 3
Outputs:
- layer_out: bfloat16 [32, 1024, 768], P(('dp', 'fsdp'))
- tokens_grad: bfloat16 [32, 1024, 768], P(('dp', 'fsdp'))
- grad_w_qkv: float32 [768, 2304], P(('dp', 'fsdp'))
- grad_b_qv: float32 [1536], P(('dp', 'fsdp'))
- grad_w_out: float32 [768, 768], P(('dp', 'fsdp'))
- grad_b_out: float32 [768], P(('dp', 'fsdp'))
- grad_ln1_gain: float32 [768], P(('dp', 'fsdp'))
- grad_ln1_bias: float32 [768], P(('dp', 'fsdp'))
- grad_w_up: float32 [768, 3072], P(('dp', 'fsdp'))
- grad_b_up: float32 [3072], P(('dp', 'fsdp'))
- grad_w_down: float32 [3072, 768], P(('dp', 'fsdp'))
- grad_b_down: float32 [768], P(('dp', 'fsdp'))
- grad_ln2_gain: float32 [768], P(('dp', 'fsdp'))
- grad_ln2_bias: float32 [768], P(('dp', 'fsdp'))
- grad_w_pool: float32 [768, 768], P(('dp', 'fsdp'))
- grad_b_pool: float32 [768], P(('dp', 'fsdp'))
- loss: float32 [], replicated
Inputs may be any that keep to these rules, and one draw needn't show every extreme that they name: partners[partners[i]] = i and partners[i] != i: the 32 views form 32 / 2 pairs. lengths[partners[i]] = lengths[i]; the longest view has exactly 1024 live tokens.
All inputs are finite; a program needn't handle non-finite values. No bound on the sum of `keep_attn` or of `keep_ffn` on one device may be relied on, other than what follows from the above.
Results may differ from a plain program's by a relative error of at most 0.029.
Values may be sent and summed in bfloat16 or wider, within the bound.
A program may use at most 256 MiB of HBM per device.

v0:
```python
import functools
import math

import jax
import jax.numpy as jnp
from jax import lax
from jax.experimental import pallas as pl
from jax.experimental.pallas import tpu as pltpu
from jax.sharding import PartitionSpec as P

HEAD_DIM = 64
LANES = 128
f32, bf16 = jnp.float32, jnp.bfloat16
MESH = pl.DeviceIdType.MESH
AXES = ("dp", "fsdp")
eps_norm = 1e-05
keep_scale = 1.0 / 0.9
logit_divisor = 0.05
neg_fill = -1000000000.0
VMEM_LIMIT = 67043328
DIMS = ("z", "c", "y", "x")
GATHER_ORDERS = (
    ("z", "x", "y", "c"),
    ("x", "z", "y", "c"),
    ("z", "y", "x", "c"),
    ("z", "y", "x", "c"),
    ("y", "z", "x", "c"),
    ("z", "x", "y", "c"),
)
SCATTER_ORDERS = (("c", "y", "x", "z"), ("c", "x", "y", "z"))
LAG = 2


class Grid:
    def __init__(self, mesh, with_fsdp=True):
        dp, fsdp = mesh.shape["dp"], mesh.shape["fsdp"]
        cores = 2 if dp % 2 == 0 else 1
        side = math.isqrt(fsdp)
        if side * side != fsdp:
            side = fsdp
        self.with_fsdp = with_fsdp
        self.size = {
            "z": dp // cores,
            "c": cores,
            "y": fsdp // side if with_fsdp else 1,
            "x": side if with_fsdp else 1,
        }
        self.shape = tuple(self.size[d] for d in DIMS)
        self.count = math.prod(self.shape)
        self.slots = sum(n - 1 for n in self.shape)

    def me(self):
        dp, fsdp = lax.axis_index("dp"), lax.axis_index("fsdp")
        at = {"z": lax.div(dp, self.size["c"]), "c": lax.rem(dp, self.size["c"])}
        if self.with_fsdp:
            at["y"], at["x"] = lax.div(fsdp, self.size["x"]), lax.rem(fsdp, self.size["x"])
        else:
            at["y"], at["x"] = 0, 0
        return at

    def device(self, at):
        fsdp = at["y"] * self.size["x"] + at["x"] if self.with_fsdp else lax.axis_index("fsdp")
        return (at["z"] * self.size["c"] + at["c"], fsdp)

    def peer(self, at, dim, j):
        other = dict(at)
        other[dim] = lax.rem(at[dim] + j, self.size[dim])
        return other

    def slot(self, dim, j):
        base = 0
        for d in DIMS:
            if d == dim:
                return base + j - 1
            base += self.size[d] - 1

    def order(self, order):
        return tuple(d for d in order if self.size[d] > 1)

    def straight(self):
        return [{d: j} for d in DIMS for j in range(1, self.size[d])]

    def around(self, dims):
        offsets = [{}]
        for d in dims:
            offsets = [{**o, d: j} if j else o for o in offsets for j in range(self.size[d])]
        return [o for o in offsets if o]

    def moved(self, at, offset):
        return {d: lax.rem(at[d] + offset[d], self.size[d]) if d in offset else at[d] for d in DIMS}

    def barrier(self, offsets):
        at, sem = self.me(), pltpu.get_barrier_semaphore()
        for offset in offsets:
            pl.semaphore_signal(
                sem, inc=1, device_id=self.device(self.moved(at, offset)), device_id_type=MESH
            )
        pl.semaphore_wait(sem, len(offsets))


class Exchange:
    def __init__(self, grid, ref, send, recv):
        self.grid, self.ref, self.send, self.recv, self.at = grid, ref, send, recv, grid.me()
        self.groups = [("z", "c"), ("y", "x")]

    def copies(self, stage):
        done = self.groups[0] if stage else ()
        view = self.ref.at[tuple(slice(None) if d in done else self.at[d] for d in DIMS)]
        first = len(self.grid.around(self.groups[0])) if stage else 0
        for j, offset in enumerate(self.grid.around(self.groups[stage])):
            yield pltpu.make_async_remote_copy(
                src_ref=view,
                dst_ref=view,
                send_sem=self.send.at[first + j],
                recv_sem=self.recv.at[first + j],
                device_id=self.grid.device(self.grid.moved(self.at, offset)),
                device_id_type=MESH,
            )

    def start(self, stage):
        for copy in self.copies(stage):
            copy.start()

    def wait(self, stage):
        for copy in self.copies(stage):
            copy.wait_recv()

    def finish(self):
        for stage in range(2):
            for copy in self.copies(stage):
                copy.wait_send()


class Gather:
    def __init__(self, grid, pieces, send, recv, window=4, lag=3):
        self.grid, self.send, self.recv, self.at = grid, send, recv, grid.me()
        self.pieces = [(ref, sub, grid.order(order)) for ref, sub, order in pieces]
        self.stages, self.window, self.now = len(self.pieces[0][2]), window, 0
        self.events = [
            (step - stage * lag, stage)
            for step in range(len(pieces) + (self.stages - 1) * lag)
            for stage in range(self.stages)
            if 0 <= step - stage * lag < len(pieces)
        ]
        self.whole = [self.events.index((i, self.stages - 1)) + 1 for i in range(len(pieces))]

    def copies(self, i, stage):
        ref, sub, order = self.pieces[i]
        dim, done = order[stage], order[:stage]
        index = tuple(slice(None) if d in done else self.at[d] for d in DIMS)
        view = ref.at[index + sub]
        for j in range(1, self.grid.size[dim]):
            slot = self.grid.slot(dim, j)
            yield pltpu.make_async_remote_copy(
                src_ref=view,
                dst_ref=view,
                send_sem=self.send.at[i, slot],
                recv_sem=self.recv.at[i, slot],
                device_id=self.grid.device(self.grid.peer(self.at, dim, j)),
                device_id_type=MESH,
            )

    def start(self, i, stage):
        for copy in self.copies(i, stage):
            copy.start()

    def begin(self):
        for i in range(min(self.window, len(self.pieces))):
            self.start(i, 0)

    def run(self, first, last):
        for i, stage in self.events[first:last]:
            for copy in self.copies(i, stage):
                copy.wait_recv()
            if stage == 0 and i + self.window < len(self.pieces):
                self.start(i + self.window, 0)
            if stage < self.stages - 1:
                self.start(i, stage + 1)

    def until(self, last):
        self.run(self.now, max(self.now, last))
        self.now = max(self.now, last)

    def finish(self):
        self.until(len(self.events))
        for i in range(len(self.pieces)):
            for stage in range(self.stages):
                for copy in self.copies(i, stage):
                    copy.wait_send()

    def loop(self, count, marks, body):
        marks = [max(self.now, m) for m in marks]
        starts = [self.now] + marks[:-1]

        def step(t, _):
            for k in range(count):
                if marks[k] > starts[k]:

                    @pl.when(t == k)
                    def _():
                        self.run(starts[k], marks[k])

            body(t)
            return 0

        lax.fori_loop(0, count, step, 0)
        self.now = marks[-1]


class Scatter:
    def __init__(self, grid, pieces, send, recv):
        self.grid, self.send, self.recv, self.at = grid, send, recv, grid.me()
        self.pieces = [(src, sub, grid.order(order), bufs, out) for src, sub, order, bufs, out in pieces]
        self.stages = len(self.pieces[0][2])
        self.steps = len(pieces) + (self.stages - 1) * LAG

    def pick(self, i, stage, where):
        src, sub, order, bufs, _ = self.pieces[i]
        left = tuple(d for d in DIMS if d not in order[:stage])
        index = tuple(where if d == order[stage] else slice(None) for d in left)
        if stage == 0:
            return src.at[index + sub]
        return bufs[stage - 1].at[(0,) + index]

    def copies(self, i, stage):
        _, _, order, bufs, _ = self.pieces[i]
        dim = order[stage]
        for j in range(1, self.grid.size[dim]):
            other = self.grid.peer(self.at, dim, j)
            slot = self.grid.slot(dim, j)
            yield pltpu.make_async_remote_copy(
                src_ref=self.pick(i, stage, other[dim]),
                dst_ref=bufs[stage].at[j - 1],
                send_sem=self.send.at[i, slot],
                recv_sem=self.recv.at[i, slot],
                device_id=self.grid.device(other),
                device_id_type=MESH,
            )

    def begin(self, i):
        for copy in self.copies(i, 0):
            copy.start()

    def run(self, first, last):
        for step in range(first, last):
            for stage in range(self.stages):
                i = step - stage * LAG
                if 0 <= i < len(self.pieces):
                    self.add(i, stage)
                    if stage < self.stages - 1:
                        for copy in self.copies(i, stage + 1):
                            copy.start()

    def add(self, i, stage):
        _, _, order, bufs, out = self.pieces[i]
        for copy in self.copies(i, stage):
            copy.wait_recv()
        buf = bufs[stage]
        total = self.pick(i, stage, self.at[order[stage]])[...].astype(f32)
        for j in range(self.grid.size[order[stage]] - 1):
            total = total + buf[j].astype(f32)
        if stage == self.stages - 1:
            out[...] = total.reshape(out.shape)
        else:
            buf[0] = total.astype(buf.dtype)

    def finish(self):
        for i in range(len(self.pieces)):
            for stage in range(self.stages):
                for copy in self.copies(i, stage):
                    copy.wait_send()


def scatter_buffers(grid, order, rows, columns, dtype):
    shapes, left = [], list(DIMS)
    for d in grid.order(order):
        left.remove(d)
        shapes.append((grid.size[d] - 1,) + tuple(grid.size[e] for e in left) + (rows, columns))
    return [pltpu.VMEM(s, dtype) for s in shapes]


def cuts(total, parts, unit):
    while parts > 1 and total % (parts * unit):
        parts -= 1
    return [(j * (total // parts), total // parts) for j in range(parts)]


def dotg(a, b, ca, cb, precision=None):
    return lax.dot_general(
        a, b, (((ca,), (cb,)), ((), ())), preferred_element_type=f32, precision=precision
    )


def iota(shape, dim):
    return lax.broadcasted_iota(jnp.int32, shape, dim)


def three_parts(x):
    high = x.astype(bf16).astype(f32)
    mid = (x - high).astype(bf16).astype(f32)
    return high, mid, x - high - mid


def spread_vector(rows, n):
    shards, width = rows.shape
    total = shards * n
    place = (iota((width, total), 1) % n == iota((width, total), 0)).astype(f32).astype(bf16)
    wide = dotg(rows, place, 1, 0)
    keep = iota((shards, total), 1) // n == iota((shards, total), 0)
    return jnp.sum(jnp.where(keep, wide, 0.0), axis=0, keepdims=True)


def fold_vector(vector, shards, n, width):
    total = shards * n
    keep = iota((shards, total), 1) // n == iota((shards, total), 0)
    place = (iota((total, width), 0) % n == iota((total, width), 1)).astype(f32).astype(bf16)
    parts = [jnp.where(keep, part, 0.0).astype(bf16) for part in three_parts(vector)]
    return sum(dotg(part, place, 1, 0) for part in parts)


def attend_prepare(qkv_ref, prep, live, pair):
    length, width = qkv_ref.shape[0], qkv_ref.shape[1] // 3
    k = qkv_ref[:, pl.ds(pl.multiple_of(width + pair * LANES, LANES), LANES)].astype(f32)
    v = qkv_ref[:, pl.ds(pl.multiple_of(2 * width + pair * LANES, LANES), LANES)].astype(f32)
    lane, row = iota((length, LANES), 1), iota((length, LANES), 0)
    bias = jnp.where(row < live, 0.0, neg_fill)
    k = k * (1.0 / math.sqrt(HEAD_DIM))
    for h in range(2):
        mine, spare = lane // HEAD_DIM == h, HEAD_DIM * (1 - h)
        prep[h, 0] = jnp.where(mine, k, jnp.where(lane == spare, bias, 0.0)).astype(bf16)
        prep[h, 1] = jnp.where(mine, v, 1.0).astype(bf16)


def attend(qkv_ref, context_ref, lse_ref, prep, pair, rows, block):
    out = pl.ds(pl.multiple_of(pair * LANES, LANES), LANES)
    q = qkv_ref[rows, out].astype(f32)
    lane = iota((block, LANES), 1)
    low = lane < HEAD_DIM
    sums, tops = [], []
    for h in range(2):
        spare = HEAD_DIM * (1 - h)
        query = jnp.where(lane // HEAD_DIM == h, q, jnp.where(lane == spare, 1.0, 0.0)).astype(bf16)
        scores = dotg(query, prep[h, 0], 1, 1)
        top = jnp.max(scores, axis=1, keepdims=True)
        weights = jnp.exp(scores - top).astype(bf16)
        sums.append(dotg(weights, prep[h, 1], 1, 0))
        tops.append(top)
    num = jnp.where(low, sums[0], sums[1])
    den = pltpu.roll(jnp.where(low, sums[1], sums[0]), HEAD_DIM, 1)
    context_ref[rows, out] = (num / den).astype(bf16)
    total = jnp.where(low, tops[0], tops[1]) + jnp.log(den)
    other = pltpu.roll(total, HEAD_DIM, 1)
    kept = jnp.where(lane == 2 * pair + 1, other, lse_ref[rows, :])
    lse_ref[rows, :] = jnp.where(lane == 2 * pair, total, kept)


def gelu_parts(x):
    cdf = 0.5 * (1.0 + lax.erf(x * (1.0 / math.sqrt(2.0))))
    return cdf, jnp.exp(-0.5 * x * x) * (1.0 / math.sqrt(2.0 * math.pi))


def normalize(values):
    center = values - jnp.mean(values, axis=-1, keepdims=True)
    scale = lax.rsqrt(jnp.mean(center * center, axis=-1, keepdims=True) + eps_norm)
    return center * scale, scale


def gather_plan(shapes):
    plan, every = [("s", ())], slice(None)
    width = shapes["o"][1]
    for a, n in cuts(width, 3, LANES):
        plan += [("q", (every, pl.ds(part * width + a, n))) for part in range(3)]
    for name, parts in (("o", 2), ("u", 6), ("p", 2), ("d", 3)):
        rows, columns = shapes[name]
        for a, n in cuts(columns, parts, LANES):
            for b, m in cuts(rows, 2 if name == "d" else 1, 8):
                plan.append((name, (pl.ds(b, m) if name == "d" else every, pl.ds(a, n))))
    return [(name, sub, GATHER_ORDERS[i % len(GATHER_ORDERS)]) for i, (name, sub) in enumerate(plan)]


def forward_kernel(grid, plan, sizes, *refs):
    (len_ref, tokens_ref, keep_a, keep_f, wq, wo, wu, wd, wp), refs = refs[:9], refs[9:]
    count = len(sizes)
    small_in, refs = refs[:count], refs[count:]
    kept_hbm, (act_t, slope), refs = refs[:16], refs[16:18], refs[18:]
    firsts, small_out, refs = refs[0], refs[1 : 1 + count], refs[1 + count :]
    kept, refs = refs[:16], refs[16:]
    (gq, go, gu, gd, gp, qkv_ref, context, lse, tokens_t, context_t, hidden_t, norm1, scale1, norm2, scale2, layer_out) = kept
    (gs, keep, hidden, hidden_low, act, act_buf, slope_buf, prep, bias), refs = refs[:9], refs[9:]
    send, recv, own_sem, keep_sem, act_sem, slope_sem, out_sem = refs
    length, width = context.shape
    b_qv, b_out, g1, b1, b_up, b_down, g2, b2, b_pool = small_out
    outs = [pltpu.make_async_copy(src, dst, out_sem.at[i]) for i, (src, dst) in enumerate(zip(kept, kept_hbm))]

    def put(*which):
        for i, ref in enumerate(kept):
            if any(ref is w for w in which):
                outs[i].start()

    at = grid.me()
    own = tuple(at[d] for d in DIMS)
    load = pltpu.make_async_copy(keep_a, keep, keep_sem)
    load.start()
    to_own = []
    for i, (src, dst) in enumerate(((wq, gq), (wo, go), (wu, gu), (wd, gd), (wp, gp))):
        to_own.append(pltpu.make_async_copy(src, dst.at[own], own_sem.at[i]))
        to_own[-1].start()
    mine = gs.at[own]
    mine[...] = jnp.zeros(mine.shape, bf16)
    for i, (ref, n) in enumerate(zip(small_in, sizes)):
        mine[i : i + 1, 0:n] = ref[...]
    where = dict(q=gq, o=go, u=gu, d=gd, p=gp, s=gs)
    gather = Gather(grid, [(where[name], sub, order) for name, sub, order in plan], send, recv)
    number = {}
    for i, (name, _, _) in enumerate(plan):
        number.setdefault(name, []).append(i)
    end = {name: [gather.whole[i] for i in numbers] for name, numbers in number.items()}
    grid.barrier(grid.straight())
    for copy in to_own:
        copy.wait()
    gather.begin()
    tokens_t[...] = tokens_ref[...].T
    lse[...] = jnp.zeros_like(lse)
    put(tokens_t)
    gather.until(end["s"][0])
    rows = gs[...].reshape((grid.count,) + gs.shape[-2:])
    for i, (ref, n) in enumerate(zip(small_out, sizes)):
        ref[...] = spread_vector(rows[:, i, :], n)
    bias[:, :width] = b_qv[:, :width]
    bias[:, width : 2 * width] = jnp.zeros((1, width), f32)
    bias[:, 2 * width :] = b_qv[:, width:]

    groups = len(number["q"]) // 3
    part = width // groups
    pairs, block = part // LANES, min(512, length)
    blocks, live = length // block, len_ref[0]
    each = pairs * blocks

    def attention(t):
        @pl.when(t % each == 0)
        def _():
            for j in range(3):
                cols = pl.ds(pl.multiple_of(j * width + t // each * part, part), part)
                out = dotg(tokens_ref[...], gq[:, :, :, :, :, cols].reshape(width, part), 1, 0)
                qkv_ref[:, cols] = (out + bias[:, cols]).astype(bf16)

        @pl.when(t % blocks == 0)
        def _():
            attend_prepare(qkv_ref, prep, live, t // blocks)

        rows = pl.ds(pl.multiple_of((t % blocks) * block, block), block)
        attend(qkv_ref, context, lse, prep, t // blocks, rows, block)

    slots = groups * each
    first, last = end["q"][2], end["u"][len(end["u"]) // 2]
    gather.loop(
        slots,
        [max(end["q"][3 * (t // each) + 2], first + t * (last - first) // slots) for t in range(slots)],
        attention,
    )
    put(gq, qkv_ref, context, lse)

    load.wait()
    block = min(512, length)
    blocks = length // block

    def row_block(t):
        return pl.ds(pl.multiple_of(t * block, block), block)

    gather.until(end["o"][-1])

    def project(t):
        here = row_block(t)
        attended = dotg(context[here, :], go[...].reshape(width, width), 1, 0) + b_out[...]
        total = tokens_ref[here, :].astype(f32) + attended * (keep[here, :].astype(f32) * keep_scale)
        norm, scale = normalize(total)
        out = norm * g1[...] + b1[...]
        hidden[here, :] = out
        hidden_low[here, :] = out.astype(bf16)
        hidden_t[:, here] = out.astype(bf16).T
        context_t[:, here] = context[here, :].T
        norm1[here, :] = norm.astype(bf16)
        scale1[here, :] = jnp.broadcast_to(scale, (block, LANES))

    gather.loop(blocks, [gather.now] * blocks, project)
    load = pltpu.make_async_copy(keep_f, keep, keep_sem)
    load.start()
    put(go, hidden_t, context_t, norm1, scale1)

    parts = len(end["u"])
    step = gu.shape[-1] // parts
    strip = min(128, length)

    def saved(t, cols):
        yield pltpu.make_async_copy(act_buf.at[t % 2], act_t.at[cols, :], act_sem.at[t % 2])
        yield pltpu.make_async_copy(slope_buf.at[t % 2], slope.at[:, cols], slope_sem.at[t % 2])

    def up(t):
        cols = pl.ds(pl.multiple_of(t * step, step), step)
        weight = gu[:, :, :, :, :, cols].reshape(width, step)

        @pl.when(t >= 2)
        def _():
            for copy in saved(t, cols):
                copy.wait()

        for i in range(length // strip):
            here = slice(i * strip, (i + 1) * strip)
            pre = dotg(hidden_low[here, :], weight, 1, 0) + b_up[:, cols]
            cdf, pdf = gelu_parts(pre)
            out = (pre * cdf).astype(bf16)
            act[here, cols] = out
            act_buf[t % 2, :, here] = out.T
            slope_buf[t % 2, here, :] = (cdf + pre * pdf).astype(bf16)
        for copy in saved(t, cols):
            copy.start()

    gather.loop(parts, end["u"], up)
    for t in range(max(0, parts - 2), parts):
        for copy in saved(t, pl.ds(0, step)):
            copy.wait()

    load.wait()
    put(gu)
    halves = len(cuts(gd.shape[-2], 2, 8))
    ends = end["d"][halves - 1 :: halves]
    parts = len(ends)
    step = width // parts

    def down(t):
        cols = pl.ds(pl.multiple_of(t * step, step), step)
        out = dotg(act[...], gd[:, :, :, :, :, cols].reshape(-1, step), 1, 0) + b_down[:, cols]
        hidden[:, cols] += out * (keep[:, cols].astype(f32) * keep_scale)

    gather.loop(parts, ends, down)
    put(gd, gp)
    block = min(256, length)
    blocks = length // block

    def norm(t):
        here = row_block(t)
        value, scale = normalize(hidden[here, :])
        out = value * g2[...] + b2[...]
        norm2[here, :] = value.astype(bf16)
        scale2[here, :] = jnp.broadcast_to(scale, (block, LANES))
        layer_out[here, :] = out.astype(bf16)

        @pl.when(t == 0)
        def _():
            first = out[0:8].astype(bf16)
            pooled = jnp.tanh(dotg(first, gp[...].reshape(width, width), 1, 0) + b_pool[...])
            firsts[0:1, :] = pooled[0:1]
            firsts[1:2, :] = first[0:1].astype(f32)

    gather.loop(blocks, [gather.now] * blocks, norm)
    put(norm2, scale2, layer_out)
    gather.finish()
    for copy in outs:
        copy.wait()


def run_forward(grid, length_of, tokens, keep_a, keep_f, big, small):
    length, width = tokens.shape
    names = ("q", "o", "u", "d", "p")
    shapes = {k: w.shape for k, w in zip(names, big)}
    inner = shapes["u"][1]
    sizes = [v.shape[0] for v in small]
    plan = gather_plan(shapes)
    pad = -(-max(sizes) // LANES) * LANES
    step = inner // sum(p[0] == "u" for p in plan)
    vmem, anywhere = pl.BlockSpec(memory_space=pltpu.VMEM), pl.BlockSpec(memory_space=pl.ANY)
    shape = jax.ShapeDtypeStruct
    kept = [(grid.shape + shapes[k], bf16) for k in names] + [
        ((length, 3 * width), bf16),
        ((length, width), bf16),
        ((length, LANES), f32),
        ((width, length), bf16),
        ((width, length), bf16),
        ((width, length), bf16),
        ((length, width), bf16),
        ((length, LANES), f32),
        ((length, width), bf16),
        ((length, LANES), f32),
        ((length, width), bf16),
    ]
    return pl.pallas_call(
        functools.partial(forward_kernel, grid, plan, sizes),
        out_shape=[shape(*k) for k in kept]
        + [shape((inner, length), bf16), shape((length, inner), bf16), shape((2, width), f32)]
        + [shape((1, grid.count * n), f32) for n in sizes],
        in_specs=[pl.BlockSpec(memory_space=pltpu.SMEM), vmem, anywhere, anywhere] + [vmem] * (5 + len(small)),
        out_specs=[anywhere] * 18 + [vmem] * (1 + len(small)),
        scratch_shapes=[pltpu.VMEM(*k) for k in kept]
        + [
            pltpu.VMEM(grid.shape + (16, pad), bf16),
            pltpu.VMEM((length, width), jnp.int32),
            pltpu.VMEM((length, width), f32),
            pltpu.VMEM((length, width), bf16),
            pltpu.VMEM((length, inner), bf16),
            pltpu.VMEM((2, step, length), bf16),
            pltpu.VMEM((2, length, step), bf16),
            pltpu.VMEM((2, 2, length, LANES), bf16),
            pltpu.VMEM((1, 3 * width), f32),
            pltpu.SemaphoreType.DMA((len(plan), grid.slots)),
            pltpu.SemaphoreType.DMA((len(plan), grid.slots)),
            pltpu.SemaphoreType.DMA((5,)),
            pltpu.SemaphoreType.DMA,
            pltpu.SemaphoreType.DMA((2,)),
            pltpu.SemaphoreType.DMA((2,)),
            pltpu.SemaphoreType.DMA((16,)),
        ],
        compiler_params=pltpu.CompilerParams(
            collective_id=0, has_side_effects=True, vmem_limit_bytes=VMEM_LIMIT
        ),
        name="forward",
    )(length_of, tokens, keep_a, keep_f, *big, *[v.reshape(1, -1) for v in small])


def pool_and_loss(views, partners_ref, wp, here, shard_rows, unit_ref, work, cls_grad, pool_w, pool_b, loss):
    high = lax.Precision.HIGHEST
    count, width = math.prod(views.shape[:4]), views.shape[-1]
    each = count // views.shape[0]

    def pooled_rows(z):
        rows = views[z].reshape((each,) + views.shape[-2:])
        pooled = rows[:, 0, :]
        scale = lax.rsqrt(jnp.sum(pooled * pooled, axis=1, keepdims=True) + 1e-06)
        return slice(z * each, (z + 1) * each), pooled, scale, rows[:, 1, :]

    for z in range(views.shape[0]):
        at, pooled, scale, cls = pooled_rows(z)
        unit_ref[at, :] = pooled * scale
        work[count + z * each : count + (z + 1) * each, :] = cls.astype(bf16)
    unit = unit_ref[0:count, :]
    sims = dotg(unit, unit, 1, 1, high) / logit_divisor
    column, row = iota((count, count), 1), iota((count, count), 0)
    others = jnp.where(row == column, neg_fill, sims)
    top = jnp.max(others, axis=1, keepdims=True)
    weights = jnp.exp(others - top)
    total = jnp.sum(weights, axis=1, keepdims=True)
    partner = column == partners_ref[...]
    target = jnp.sum(jnp.where(partner, sims, 0.0), axis=1, keepdims=True)
    lost = jnp.sum(top + jnp.log(total) - target, axis=0, keepdims=True) / count
    loss[...] = jnp.broadcast_to(lost, loss.shape)
    pull = weights / total - jnp.where(partner, 1.0, 0.0)
    pull = pull + dotg(pull, (row == column).astype(f32), 0, 0, high)
    for z in range(views.shape[0]):
        at, pooled, scale, _ = pooled_rows(z)
        unit_grad = dotg(pull[at], unit, 1, 0, high) / logit_divisor
        along = jnp.sum(pooled * unit_grad, axis=1, keepdims=True)
        pooled_grad = scale * unit_grad - pooled * (scale * scale * scale * along)
        work[at, :] = (pooled_grad * (1.0 - pooled * pooled)).astype(bf16)
    pre, cls = work[0:count, :], work[count : 2 * count, :]
    mine = jnp.sum(jnp.where(iota((count, width), 0) == here, pre.astype(f32), 0.0), axis=0, keepdims=True)
    cls_grad[...] = dotg(jnp.broadcast_to(mine, (8, width)).astype(bf16), wp, 1, 1)
    place = (iota((width, LANES), 0) == here * shard_rows + iota((width, LANES), 1)).astype(f32).astype(bf16)
    cls_rows = dotg(cls, place, 1, 0).astype(bf16)
    pool_w[...] = dotg(cls_rows, pre, 0, 0)[:shard_rows]
    sums = jnp.broadcast_to(jnp.sum(pre.astype(f32), axis=0, keepdims=True), (8, width))
    pool_b[...] = sum(dotg(part.astype(bf16), place, 1, 0) for part in three_parts(sums))


def attend_back(qkv_ref, context, dcontext, lse, live, pair, prep):
    length, width = qkv_ref.shape[0], context.shape[1]
    scale = 1.0 / math.sqrt(HEAD_DIM)
    one = pl.ds(pl.multiple_of(pair * LANES, LANES), LANES)

    def col(part):
        return pl.ds(pl.multiple_of(part * width + pair * LANES, LANES), LANES)

    q, k, v = (qkv_ref[:, col(j)].astype(f32) for j in range(3))
    d = dcontext[:, one].astype(f32)
    lane, row = iota((length, LANES), 1), iota((length, LANES), 0)
    bias = jnp.where(row < live, 0.0, neg_fill)
    both = d * context[:, one].astype(f32)
    for h in range(2):
        mine, a = lane // HEAD_DIM == h, HEAD_DIM * (1 - h)
        inner = jnp.sum(jnp.where(mine, both, 0.0), axis=1, keepdims=True)
        total = jnp.sum(jnp.where(lane == 2 * pair + h, lse[...], 0.0), axis=1, keepdims=True)
        l0, l1, l2 = three_parts(-total)
        d0, d1, d2 = three_parts(-inner)

        def lanes(base, *extra):
            out = 0.0
            for j, e in reversed(list(enumerate(extra))):
                out = jnp.where(lane == a + j, e, out)
            return jnp.where(mine, base, out).astype(bf16)

        prep[h, 0] = lanes(q * scale, 1.0, l0, l1, l2)
        prep[h, 1] = lanes(k, bias, 1.0, 1.0, 1.0)
        prep[h, 2] = lanes(d, d0, d1, d2)
        prep[h, 3] = lanes(v, 1.0, 1.0, 1.0)
        prep[h, 4] = lanes(k * scale)
    return (q * scale).astype(bf16).T, d.astype(bf16).T


def scatter_plan(grid, shapes):
    plan, every = [], slice(None)
    width = shapes["o"][1]
    rows, columns = shapes["d"]
    plan += [("d", (pl.ds(a, n), every), n, columns) for a, n in cuts(rows, 6, 8)]
    for name, parts in (("u", 6), ("o", 2)):
        rows, columns = shapes[name]
        plan += [(name, (every, pl.ds(a, n)), rows, n) for a, n in cuts(columns, parts, LANES)]
    for a, n in cuts(width, 3, LANES):
        plan += [("q", (every, pl.ds(part * width + a, n)), shapes["q"][0], n) for part in range(3)]
    plan.append(("s", (), 16, shapes["s"]))
    return [(p[0], p[1], SCATTER_ORDERS[i % 2]) + p[2:] for i, p in enumerate(plan)]


def backward_kernel(grid, whole, plan, sizes, shard_rows, *refs):
    (len_ref, partners_ref, firsts, g1, g2), refs = refs[:5], refs[5:]
    (h_cot, h_keep_a, h_keep_f, h_norm1, h_scale1, h_norm2, h_scale2, h_act, h_slope, h_hidden, h_context_t), refs = refs[:11], refs[11:]
    (h_qkv, h_context, h_lse, h_tokens, h_wq, h_wo, h_wu, h_wd, h_wp), refs = refs[:9], refs[9:]
    (rq, ro, ru, rd, rs, pool_w, pool_b, loss, h_tokens_grad), refs = refs[:9], refs[9:]
    (dd, du, do, dsmall, grad, gctx, low, norm, keep, scale, vec, cls_grad, views, wp), refs = refs[:14], refs[14:]
    (send, recv, view_send, view_recv, sems, pair_sems), bufs = refs[:6], list(refs[6:])
    length, width = grad.shape
    inner = vec.shape[1]
    sources, results = dict(d=dd, u=du, o=do, s=dsmall), dict(d=rd, u=ru, o=ro, q=rq, s=rs)
    number = {}
    for i, p in enumerate(plan):
        number.setdefault(p[0], []).append(i)
    cot = low

    def copy(k, src, dst):
        return pltpu.make_async_copy(src, dst, sems.at[k])

    first_loads = [copy(0, h_cot, cot), copy(1, h_norm2, norm), copy(2, h_scale2, scale), copy(3, h_keep_f, keep), copy(4, h_wp, wp)]
    for c in first_loads:
        c.start()
    at_all = whole.me()
    views[tuple(at_all[d] for d in DIMS)] = firsts[...]
    exchange = Exchange(whole, views, view_send, view_recv)
    whole.barrier(whole.straight() + [o for o in whole.around(("z", "c")) + whole.around(("y", "x")) if len(o) > 1])
    exchange.start(0)
    vec[...] = jnp.zeros_like(vec)
    for c in first_loads:
        c.wait()
    strip = min(128, length)
    strips = length // strip

    def strip_of(t):
        return pl.ds(pl.multiple_of(t * strip, strip), strip)

    def add_row(j, x):
        vec[j : j + 1, : x.shape[1]] += jnp.sum(x, axis=0, keepdims=True)

    def norm_back(here, up, gain, slot):
        value = norm[here, :].astype(f32)
        scaled = up * gain[...]
        along = jnp.mean(scaled * value, axis=1, keepdims=True)
        back = scale[here, 0:1] * (scaled - jnp.mean(scaled, axis=1, keepdims=True) - value * along)
        add_row(slot, up * value)
        add_row(slot + 1, up)
        grad[here, :] = back
        out = (back * (keep[here, :].astype(f32) * keep_scale)).astype(bf16)
        low[here, :] = out
        return out.astype(f32)

    def second_norm(t, extra):
        here = strip_of(t)
        up = cot[here, :].astype(f32)
        if extra is not None:
            up = up + jnp.where(iota((strip, width), 0) + t * strip == 0, extra, 0.0)
        add_row(5, norm_back(here, up, g2, 6))
        return 0

    held = -(-math.prod(whole.shape) // strip)
    lax.fori_loop(held, strips, lambda t, _: second_norm(t, None), 0)
    exchange.wait(0)
    exchange.start(1)
    exchange.wait(1)
    here = lax.axis_index("dp") * (whole.size["y"] * whole.size["x"]) + lax.axis_index("fsdp")
    pool_and_loss(views, partners_ref, wp[...], here, shard_rows, grad, gctx, cls_grad, pool_w, pool_b, loss)
    lax.fori_loop(0, held, lambda t, _: second_norm(t, cls_grad[0:1, :]), 0)
    wo = wp
    second_loads = [copy(1, h_norm1, norm), copy(2, h_scale1, scale), copy(3, h_keep_a, keep), copy(6, h_wo, wo)]
    for c in second_loads:
        c.start()

    pieces, left = [], bufs
    for name, sub, order, _, _ in plan:
        n = len(grid.order(order))
        pieces.append([sources.get(name), sub, order, left[:n], results[name].at[sub] if sub else results[name]])
        left = left[n:]
    scatter = Scatter(grid, pieces, send, recv)

    def feed_forward(act, slope, wd, wu, gup, turned):
        third = [copy(5, h_hidden, turned), copy(7, h_context_t, turned)]
        third[0].start()
        block = min(256, length)
        chunk, part = act.shape[1], slope.shape[2]
        chunks, parts = inner // chunk, inner // part
        slab = wu.shape[1]

        def act_load(t):
            return pltpu.make_async_copy(h_act.at[pl.ds(pl.multiple_of(t * chunk, chunk), chunk), :], act.at[t % 2], pair_sems.at[0, t % 2])

        def part_loads(t):
            cols = pl.ds(pl.multiple_of(t * part, part), part)
            yield pltpu.make_async_copy(h_slope.at[:, cols], slope.at[t % 2], pair_sems.at[1, t % 2])
            yield pltpu.make_async_copy(h_wd.at[cols, :], wd.at[t % 2], pair_sems.at[2, t % 2])

        def slab_load(t):
            return pltpu.make_async_copy(h_wu.at[pl.ds(pl.multiple_of(t * slab, slab), slab), :], wu.at[t % 2], pair_sems.at[3, t % 2])

        act_load(0).start()
        for c in part_loads(0):
            c.start()
        slab_load(0).start()
        across = grid.size["y"] * grid.size["x"]

        def down_weight(t, _):
            @pl.when(t + 1 < chunks)
            def _():
                act_load(t + 1).start()

            act_load(t).wait()
            out = dotg(act[t % 2], low[...], 1, 0).astype(bf16)
            dd[t // grid.size["c"], t % grid.size["c"]] = out.reshape(dd.shape[2:])
            return 0

        lax.fori_loop(0, chunks, down_weight, 0)
        for i in number["d"]:
            scatter.begin(i)
        third[0].wait()

        def up_part(t, _):
            cols = pl.ds(pl.multiple_of(t * part, part), part)

            @pl.when(t + 1 < parts)
            def _():
                for c in part_loads(t + 1):
                    c.start()

            for c in part_loads(t):
                c.wait()
            for i in range(length // block):
                rows = slice(i * block, (i + 1) * block)
                out = dotg(low[rows, :], wd[t % 2], 1, 1) * slope[t % 2, rows, :].astype(f32)
                gup[rows, cols] = out.astype(bf16)
            vec[4:5, cols] = jnp.sum(gup[:, cols].astype(f32), axis=0, keepdims=True)
            out = dotg(turned[...], gup[:, cols], 1, 0).astype(bf16)
            du[:, :, :, :, :, cols] = out.reshape(grid.shape + (-1, part))
            for k, i in enumerate(number["u"]):

                @pl.when(t == k)
                def _():
                    scatter.begin(i)
                    scatter.run(k, k + 1)

            return 0

        lax.fori_loop(0, parts, up_part, 0)
        third[1].start()

        def hidden_part(t, _):
            cols = pl.ds(pl.multiple_of(t * slab, slab), slab)

            @pl.when(t + 1 < width // slab)
            def _():
                slab_load(t + 1).start()

            slab_load(t).wait()
            grad[:, cols] += dotg(gup[...], wu[t % 2], 1, 1)
            for k in range(width // slab):

                @pl.when(t == k)
                def _():
                    scatter.run(parts + k, parts + k + 1)

            return 0

        lax.fori_loop(0, width // slab, hidden_part, 0)
        for c in second_loads:
            c.wait()

        def first_norm(t, _):
            add_row(1, norm_back(strip_of(t), grad[strip_of(t), :], g1, 2))
            return 0

        lax.fori_loop(0, strips, first_norm, 0)
        third[1].wait()
        for i in number["o"]:
            cols = plan[i][1][1]
            out = dotg(turned[...], low[:, cols], 1, 0).astype(bf16)
            do[:, :, :, :, :, cols] = out.reshape(grid.shape + (-1, cols.size))
            scatter.begin(i)
        for i in range(length // block):
            rows = slice(i * block, (i + 1) * block)
            gctx[rows, :] = dotg(low[rows, :], wo[...], 1, 1).astype(bf16)
        scatter.run(parts + width // slab, parts + width // slab + 1)
        return parts + width // slab + 1

    chunk, part, slab = inner // (grid.size["z"] * grid.size["c"]), inner // len(number["u"]), width // 3
    done = []

    def first_scope(*refs):
        done.append(feed_forward(*refs))

    pl.run_scoped(
        first_scope,
        pltpu.VMEM((2, chunk, length), bf16),
        pltpu.VMEM((2, length, part), bf16),
        pltpu.VMEM((2, part, width), bf16),
        pltpu.VMEM((2, slab, inner), bf16),
        pltpu.VMEM((length, inner), bf16),
        pltpu.VMEM((width, length), bf16),
    )
    step = done[0]

    def attention(qkv, lse, tokens_t, wq, dq, prep, turned, acc):
        context = norm
        block = min(256, length) if grid.with_fsdp else min(128, length)
        blocks = length // block

        def rows_of(t):
            return pl.ds(pl.multiple_of(t * block, block), block)

        for i in number["q"]:
            scatter.pieces[i] = (dq,) + scatter.pieces[i][1:]
        loads = [copy(8, h_qkv, qkv), copy(9, h_context, context), copy(10, h_lse, lse), copy(11, h_tokens, tokens_t), copy(12, h_wq.at[:, 0:width], wp), copy(6, h_wq.at[:, width : 2 * width], wq.at[0]), copy(7, h_wq.at[:, 2 * width :], wq.at[1])]
        for c in loads:
            c.start()
        for c in loads[:3]:
            c.wait()
        groups = len(number["q"]) // 3
        span = width // groups
        each = span // LANES * blocks
        slots = groups * each
        live = len_ref[0]
        head = [slice(h * HEAD_DIM, (h + 1) * HEAD_DIM) for h in range(2)]
        marks = []
        for g in range(groups):
            lo, hi = (step if g == 0 else number["q"][3 * g - 3]), number["q"][3 * g]
            marks += [(lo + j * (hi - lo) // each, lo + (j + 1) * (hi - lo) // each) for j in range(each)]

        def slot(t, _):
            pair, b = t // blocks, t % blocks
            rows = rows_of(b)
            one = pl.ds(pl.multiple_of(pair * LANES, LANES), LANES)

            @pl.when(b == 0)
            def _():
                turned[0], turned[1] = attend_back(qkv, context, gctx, lse, live, pair, prep)
                acc[...] = jnp.zeros_like(acc)

            dq_rows = jnp.zeros((block, LANES), f32)
            for h in range(2):
                p = jnp.exp(dotg(prep[h, 0, rows, :], prep[h, 1], 1, 1))
                dp = dotg(prep[h, 2, rows, :], prep[h, 3], 1, 1)
                ds = (p * dp).astype(bf16)
                acc[0, head[h], :] += dotg(turned[1, head[h], rows], p.astype(bf16), 1, 0)
                acc[1, head[h], :] += dotg(turned[0, head[h], rows], ds, 1, 0)
                dq_rows = dq_rows + dotg(ds, prep[h, 4], 1, 0)
            qkv[rows, one] = dq_rows.astype(bf16)

            @pl.when(b == blocks - 1)
            def _():
                qkv[:, pl.ds(pl.multiple_of(width + pair * LANES, LANES), LANES)] = acc[1].astype(bf16).T
                qkv[:, pl.ds(pl.multiple_of(2 * width + pair * LANES, LANES), LANES)] = acc[0].astype(bf16).T

            for k in range(slots):
                if marks[k][1] > marks[k][0]:

                    @pl.when(t == k)
                    def _():
                        scatter.run(*marks[k])

            @pl.when(t == each - 1)
            def _():
                loads[3].wait()

            @pl.when(t % each == each - 1)
            def _():
                for j in range(3):
                    cols = pl.ds(pl.multiple_of(j * width + t // each * span, LANES), span)
                    out = dotg(tokens_t[...], qkv[:, cols], 1, 0).astype(bf16)
                    dq[:, :, :, :, :, cols] = out.reshape(grid.shape + (-1, span))
                for g in range(groups):

                    @pl.when(t == each * (g + 1) - 1)
                    def _():
                        for i in number["q"][3 * g : 3 * g + 3]:
                            scatter.begin(i)

            return 0

        lax.fori_loop(0, slots, slot, 0)
        sums = dotg(jnp.ones((8, length), bf16), qkv[...], 1, 0)[0:1]
        vec[0:1, :width] = sums[:, :width]
        vec[0:1, width : 2 * width] = sums[:, 2 * width :]
        pad = dsmall.shape[-1]
        dsmall[...] = jnp.zeros_like(dsmall)
        for j, n in enumerate(sizes):
            folded = fold_vector(vec[j : j + 1, : grid.count * n], grid.count, n, pad)
            dsmall[:, :, :, :, j, :] = folded.reshape(grid.shape + (pad,))
        scatter.begin(number["s"][0])
        at_step = number["q"][-3]
        for c in loads[4:]:
            c.wait()
        rest, parts = scatter.steps - at_step, 4
        rows = length // parts
        for i in range(parts):
            scatter.run(at_step + i * rest // parts, at_step + (i + 1) * rest // parts)
            here = slice(i * rows, (i + 1) * rows)
            total = grad[here, :] + dotg(qkv[here, :width], wp[...], 1, 1)
            for j in range(2):
                total = total + dotg(qkv[here, (j + 1) * width : (j + 2) * width], wq[j], 1, 1)
            low[here, :] = total.astype(bf16)
        out = copy(13, low, h_tokens_grad)
        out.start()
        scatter.finish()
        exchange.finish()
        out.wait()

    pl.run_scoped(
        attention,
        pltpu.VMEM((length, 3 * width), bf16),
        pltpu.VMEM((length, LANES), f32),
        pltpu.VMEM((width, length), bf16),
        pltpu.VMEM((2, width, width), bf16),
        pltpu.VMEM(grid.shape + (width // grid.count, 3 * width), bf16),
        pltpu.VMEM((2, 5, length, LANES), bf16),
        pltpu.VMEM((2, LANES, length), bf16),
        pltpu.VMEM((2, LANES, length), f32),
    )


def run_backward(grid, whole, length_of, partners, firsts, gains, hbm, length, width, inner, sizes, shard_rows):
    rows = width // grid.count
    pad = -(-max(sizes) // LANES) * LANES
    shapes = {"q": (rows, 3 * width), "o": (rows, width), "u": (rows, inner), "d": (inner // grid.count, width), "s": pad}
    plan = scatter_plan(grid, shapes)
    bufs = []
    for name, _, order, r, c in plan:
        bufs += scatter_buffers(grid, order, r, c, f32 if name == "s" else bf16)
    views_count = len(whole.around(("z", "c"))) + len(whole.around(("y", "x")))
    vmem, anywhere = pl.BlockSpec(memory_space=pltpu.VMEM), pl.BlockSpec(memory_space=pl.ANY)
    shape = jax.ShapeDtypeStruct
    return pl.pallas_call(
        functools.partial(backward_kernel, grid, whole, plan, sizes, shard_rows),
        out_shape=[shape(shapes[k], f32) for k in ("q", "o", "u", "d")]
        + [
            shape((16, pad), f32),
            shape((shard_rows, width), f32),
            shape((8, LANES), f32),
            shape((8, LANES), f32),
            shape((length, width), bf16),
        ],
        in_specs=[pl.BlockSpec(memory_space=pltpu.SMEM)] + [vmem] * 4 + [anywhere] * len(hbm),
        out_specs=[vmem] * 8 + [anywhere],
        scratch_shapes=[pltpu.VMEM(grid.shape + shapes[k], bf16) for k in ("d", "u", "o")]
        + [
            pltpu.VMEM(grid.shape + (16, pad), f32),
            pltpu.VMEM((length, width), f32),
            pltpu.VMEM((length, width), bf16),
            pltpu.VMEM((length, width), bf16),
            pltpu.VMEM((length, width), bf16),
            pltpu.VMEM((length, width), jnp.int32),
            pltpu.VMEM((length, LANES), f32),
            pltpu.VMEM((16, inner), f32),
            pltpu.VMEM((8, width), f32),
            pltpu.VMEM(whole.shape + (2, width), f32),
            pltpu.VMEM((width, width), bf16),
            pltpu.SemaphoreType.DMA((len(plan), grid.slots)),
            pltpu.SemaphoreType.DMA((len(plan), grid.slots)),
            pltpu.SemaphoreType.DMA((views_count,)),
            pltpu.SemaphoreType.DMA((views_count,)),
            pltpu.SemaphoreType.DMA((14,)),
            pltpu.SemaphoreType.DMA((4, 2)),
        ]
        + bufs,
        compiler_params=pltpu.CompilerParams(
            collective_id=1, has_side_effects=True, vmem_limit_bytes=VMEM_LIMIT
        ),
        name="backward",
    )(length_of, partners.reshape(-1, 1), firsts, *gains, *hbm)


def on_device(whole, grid, tokens, lengths, keep_attn, keep_ffn, partners, out_cot, *weights):
    (w_qkv, b_qv, w_out, b_out, ln1_gain, ln1_bias, w_up, b_up, w_down, b_down, ln2_gain, ln2_bias, w_pool, b_pool) = weights
    _, length, width = tokens.shape
    inner = w_up.shape[1]
    big = [w_qkv, w_out, w_up, w_down, w_pool]
    small = [b_qv, b_out, ln1_gain, ln1_bias, b_up, b_down, ln2_gain, ln2_bias, b_pool]
    shard_rows = w_qkv.shape[0]
    if not grid.with_fsdp:
        big = [lax.all_gather(w, "fsdp", axis=0, tiled=True) for w in big]
        small = [lax.all_gather(v, "fsdp", axis=0, tiled=True) for v in small]
    sizes = [v.shape[0] for v in small][:-1]
    flat = (length, width)
    keep_a, keep_f = keep_attn.reshape(flat), keep_ffn.reshape(flat)
    outs = run_forward(grid, lengths, tokens.reshape(flat), keep_a, keep_f, big, small)
    wq, wo, wu, wd, wp = (g.reshape(-1, g.shape[-1]) for g in outs[:5])
    qkv, context, lse, tokens_t, context_t, hidden_t, norm1, scale1, norm2, scale2, layer_out = outs[5:16]
    act_t, slope, firsts = outs[16:19]
    vectors = outs[19:]
    hbm = [
        out_cot.reshape(flat), keep_a, keep_f, norm1, scale1, norm2, scale2, act_t, slope, hidden_t, context_t,
        qkv, context, lse, tokens_t, wq, wo, wu, wd, wp,
    ]
    rq, ro, ru, rd, rs, pool_w, pool_b, loss, tokens_grad = run_backward(
        grid, whole, lengths, partners, firsts, [vectors[2], vectors[6]], hbm, length, width, inner, sizes, shard_rows
    )
    owned = [rq, ro, ru, rd] + [rs[j, :n] for j, n in enumerate(sizes)]
    if not grid.with_fsdp:
        owned = [lax.psum_scatter(g, "fsdp", scatter_dimension=0, tiled=True) for g in owned]
    rq, ro, ru, rd, s_qv, s_out, s_g1, s_b1, s_up, s_down, s_g2, s_b2 = owned
    return (
        layer_out.reshape(tokens.shape), tokens_grad.reshape(tokens.shape), rq, s_qv, ro, s_out, s_g1, s_b1, ru, s_up,
        rd, s_down, s_g2, s_b2, pool_w, pool_b[0, :shard_rows], loss[0, 0],
    )


def solution(mesh):
    rows, vector, matrix = P(AXES, None, None), P(AXES), P(AXES, None)
    weights = (matrix, vector, matrix, vector, vector, vector, matrix, vector, matrix, vector, vector, vector, matrix, vector)
    devices = mesh.shape["dp"] * mesh.shape["fsdp"]

    def step(*args):
        whole = Grid(mesh)
        grid = whole if (args[6].shape[0] // devices) % 8 == 0 else Grid(mesh, False)
        return jax.shard_map(
            functools.partial(on_device, whole, grid),
            mesh=mesh,
            in_specs=(rows, vector, rows, rows, P(), rows) + weights,
            out_specs=(rows, rows) + weights + (P(),),
            check_vma=False,
        )(*args)

    return step
```

profile of v0, /device:TPU:0, one launch (start us, length us, event | category | flops | bytes accessed | tf_op | source)
XLA Modules:
  0.0 257.5 jit_solution(7497859452935380759)
XLA Ops:
  1.3 1.3 copy.37.refs_1_
  2.6 98.4 %forward.1 = (bf16[4,2,2,2,24,2304]{5,4,3,2,1,0:T(8,128)(2,1)}, bf16[4,2,2,2,24,768]{5,4,3,2,1,0:T(8,128)(2,1)}, bf16[4,2,2,2,24,3072]{5,4,3,2,1,0:T(8,128)(2,1)...) custom-call(s32[1]{0:T(128)S(6)} %copy.45.refs_0_, ...), custom_call_target="tpu_custom_call" | custom-call | tf_op jit(solution)/shard_map/forward/pallas_call | solution.py:586
  101.1 144.1 %backward.1 = (f32[24,2304]{1,0:T(8,128)}, f32[24,768]{1,0:T(8,128)}, f32[24,3072]{1,0:T(8,128)}, f32[96,768]{1,0:T(8,128)}, f32[16,128]{1,0:T(8,128)}, /*index=...) custom-call(s32[1]{0:T(128)S(6)} %copy.45.refs_0_, s32[32,1]{1,0:T(8,128)} %copy.37.refs_1_, ...), custom_call_target="tpu_custom_call" | custom-call | tf_op jit(solution)/shard_map/backward/pallas_call | solution.py:1042
  245.2 1.2 slice.39
  246.4 1.2 slice_bitcast_fusion.4
  247.6 1.2 slice_bitcast_fusion.8
  248.8 1.4 slice_bitcast_fusion.1
  250.2 0.0 copy-start
  250.2 2.8 %copy.46 = bf16[1,1024,768]{2,1,0:T(8,128)(2,1)} copy(bf16[1,1024,768]{2,1,0:T(8,128)(2,1)} %bitcast.49) | data formatting | bytes 3145728
  253.0 0.0 copy-done
  253.0 0.0 copy-start.3
  253.0 0.0 copy-start.5
  253.0 0.0 copy-start.1
  253.0 1.1 copy.47
  254.2 0.0 copy-done.3
  254.2 0.7 copy.48
  254.8 0.0 copy-done.5
  254.8 0.6 copy.49
  255.5 0.0 copy-done.2
  255.5 0.7 copy.50
  256.2 0.0 copy-done.1
  256.2 0.7 copy.51
  256.9 0.0 copy-done.4
  256.9 0.6 copy.52
  (2 shorter events, 0.0 us)
Async XLA Ops:
  250.2 2.8 %copy-start = (bf16[1024,768]{1,0:T(8,128)(2,1)S(1)}, bf16[1024,768]{1,0:T(8,128)(2,1)}, u32[]{:S(2)}) copy-start(bf16[1024,768]{1,0:T(8,128)(2,1)} %get-tuple-element.68) | copy-start | bytes 4718596
  253.0 1.2 copy-start.3
  253.0 1.9 copy-start.5
  253.0 2.5 copy-start.2
  253.0 3.2 %copy-start.1 = (f32[96,768]{1,0:T(8,128)S(1)}, f32[96,768]{1,0:T(8,128)}, u32[]{:S(2)}) copy-start(f32[96,768]{1,0:T(8,128)} %get-tuple-element.111) | copy-start | bytes 884740
  254.2 2.8 %copy-start.4 = (f32[24,768]{1,0:T(8,128)S(1)}, f32[24,768]{1,0:T(8,128)}, u32[]{:S(2)}) copy-start(f32[24,768]{1,0:T(8,128)} %get-tuple-element.115) | copy-start | bytes 221188
where the time goes:
time: 258 us
  Pallas kernels  243 us (94%)
  local copies, waits for them, and re-layouts  13.6 us (5%)
    pallas_call x1, Pallas kernels, run_backward(): pl.pallas_call(functools.partial(backward_kernel, grid, whole, plan, size...  144 us
    pallas_call x1, Pallas kernels, run_forward(): pl.pallas_call(functools.partial(forward_kernel, grid, plan, sizes), out_...  98.4 us
    unnamed x19, local copies, waits for them, and re-layouts  7.32 us

commit v1 on v0

--- a/solution.py
+++ b/solution.py
@@ -19,6 +19,7 @@
 neg_fill = -1000000000.0
 VMEM_LIMIT = 67043328
 DIMS = ("z", "c", "y", "x")
+SPACING = 4
 GATHER_ORDERS = (
     ("z", "x", "y", "c"),
     ("x", "z", "y", "c"),
@@ -28,7 +29,6 @@
     ("z", "x", "y", "c"),
 )
 SCATTER_ORDERS = (("c", "y", "x", "z"), ("c", "x", "y", "z"))
-LAG = 2
 
 
 class Grid:
@@ -132,7 +132,7 @@
 
 
 class Gather:
-    def __init__(self, grid, pieces, send, recv, window=4, lag=3):
+    def __init__(self, grid, pieces, send, recv, window=3, lag=3):
         self.grid, self.send, self.recv, self.at = grid, send, recv, grid.me()
         self.pieces = [(ref, sub, grid.order(order)) for ref, sub, order in pieces]
         self.stages, self.window, self.now = len(self.pieces[0][2]), window, 0
@@ -212,7 +212,6 @@
         self.grid, self.send, self.recv, self.at = grid, send, recv, grid.me()
         self.pieces = [(src, sub, grid.order(order), bufs, out) for src, sub, order, bufs, out in pieces]
         self.stages = len(self.pieces[0][2])
-        self.steps = len(pieces) + (self.stages - 1) * LAG
 
     def pick(self, i, stage, where):
         src, sub, order, bufs, _ = self.pieces[i]
@@ -241,15 +240,12 @@
         for copy in self.copies(i, 0):
             copy.start()
 
-    def run(self, first, last):
-        for step in range(first, last):
-            for stage in range(self.stages):
-                i = step - stage * LAG
-                if 0 <= i < len(self.pieces):
-                    self.add(i, stage)
-                    if stage < self.stages - 1:
-                        for copy in self.copies(i, stage + 1):
-                            copy.start()
+    def run(self, events):
+        for i, stage in events:
+            self.add(i, stage)
+            if stage < self.stages - 1:
+                for copy in self.copies(i, stage + 1):
+                    copy.start()
 
     def add(self, i, stage):
         _, _, order, bufs, out = self.pieces[i]
@@ -638,7 +634,7 @@
     top = jnp.max(others, axis=1, keepdims=True)
     weights = jnp.exp(others - top)
     total = jnp.sum(weights, axis=1, keepdims=True)
-    partner = column == partners_ref[...]
+    partner = row == partners_ref[...]
     target = jnp.sum(jnp.where(partner, sims, 0.0), axis=1, keepdims=True)
     lost = jnp.sum(top + jnp.log(total) - target, axis=0, keepdims=True) / count
     loss[...] = jnp.broadcast_to(lost, loss.shape)
@@ -672,26 +668,29 @@
     d = dcontext[:, one].astype(f32)
     lane, row = iota((length, LANES), 1), iota((length, LANES), 0)
     bias = jnp.where(row < live, 0.0, neg_fill)
+    mine, place = lane // HEAD_DIM, lane % HEAD_DIM
+    source, target = iota((LANES, LANES), 0), iota((LANES, LANES), 1)
+    swap = (source // HEAD_DIM != target // HEAD_DIM).astype(f32).astype(bf16)
     both = d * context[:, one].astype(f32)
+    inner = sum(dotg(part.astype(bf16), swap, 1, 0) for part in three_parts(both))
+    d0, d1, d2 = three_parts(-inner)
+    extra_d = jnp.where(place == 0, d0, jnp.where(place == 1, d1, jnp.where(place == 2, d2, 0.0)))
+    extra_q = jnp.where(place == 0, 1.0, 0.0)
+    for j, part in enumerate(three_parts(-lse[...])):
+        head = jnp.where(target < HEAD_DIM, 2 * pair + 1, 2 * pair)
+        pick = ((source == head) & (target % HEAD_DIM == j + 1)).astype(f32).astype(bf16)
+        extra_q = extra_q + dotg(part.astype(bf16), pick, 1, 0)
+    extra_k = jnp.where(place == 0, bias, jnp.where(place < 4, 1.0, 0.0))
+    extra_v = jnp.where(place < 3, 1.0, 0.0)
+    q = q * scale
     for h in range(2):
-        mine, a = lane // HEAD_DIM == h, HEAD_DIM * (1 - h)
-        inner = jnp.sum(jnp.where(mine, both, 0.0), axis=1, keepdims=True)
-        total = jnp.sum(jnp.where(lane == 2 * pair + h, lse[...], 0.0), axis=1, keepdims=True)
-        l0, l1, l2 = three_parts(-total)
-        d0, d1, d2 = three_parts(-inner)
-
-        def lanes(base, *extra):
-            out = 0.0
-            for j, e in reversed(list(enumerate(extra))):
-                out = jnp.where(lane == a + j, e, out)
-            return jnp.where(mine, base, out).astype(bf16)
-
-        prep[h, 0] = lanes(q * scale, 1.0, l0, l1, l2)
-        prep[h, 1] = lanes(k, bias, 1.0, 1.0, 1.0)
-        prep[h, 2] = lanes(d, d0, d1, d2)
-        prep[h, 3] = lanes(v, 1.0, 1.0, 1.0)
-        prep[h, 4] = lanes(k * scale)
-    return (q * scale).astype(bf16).T, d.astype(bf16).T
+        here = mine == h
+        prep[h, 0] = jnp.where(here, q, extra_q).astype(bf16)
+        prep[h, 1] = jnp.where(here, k, extra_k).astype(bf16)
+        prep[h, 2] = jnp.where(here, d, extra_d).astype(bf16)
+        prep[h, 3] = jnp.where(here, v, extra_v).astype(bf16)
+        prep[h, 4] = jnp.where(here, k * scale, 0.0).astype(bf16)
+    return q.astype(bf16).T, d.astype(bf16).T
 
 
 def scatter_plan(grid, shapes):
@@ -784,7 +783,14 @@
         n = len(grid.order(order))
         pieces.append([sources.get(name), sub, order, left[:n], results[name].at[sub] if sub else results[name]])
         left = left[n:]
+    groups = len(number["q"]) // 3
+    early, last = len(plan) - 1 - len(number["q"]), len(plan) - 1
     scatter = Scatter(grid, pieces, send, recv)
+    stages, lag = scatter.stages, 4
+    steps = [
+        [(j - stage * lag, stage) for stage in range(stages) if 0 <= j - stage * lag < early]
+        for j in range(early + (stages - 1) * lag)
+    ]
 
     def feed_forward(act, slope, wd, wu, gup, turned):
         third = [copy(5, h_hidden, turned), copy(7, h_context_t, turned)]
@@ -848,7 +854,7 @@
                 @pl.when(t == k)
                 def _():
                     scatter.begin(i)
-                    scatter.run(k, k + 1)
+                    scatter.run(steps[k])
 
             return 0
 
@@ -868,7 +874,7 @@
 
                 @pl.when(t == k)
                 def _():
-                    scatter.run(parts + k, parts + k + 1)
+                    scatter.run(steps[parts + k])
 
             return 0
 
@@ -881,6 +887,8 @@
             return 0
 
         lax.fori_loop(0, strips, first_norm, 0)
+        for c in (copy(9, h_context, norm), copy(10, h_lse, scale)):
+            c.start()
         third[1].wait()
         for i in number["o"]:
             cols = plan[i][1][1]
@@ -890,7 +898,7 @@
         for i in range(length // block):
             rows = slice(i * block, (i + 1) * block)
             gctx[rows, :] = dotg(low[rows, :], wo[...], 1, 1).astype(bf16)
-        scatter.run(parts + width // slab, parts + width // slab + 1)
+        scatter.run(steps[parts + width // slab])
         return parts + width // slab + 1
 
     chunk, part, slab = inner // (grid.size["z"] * grid.size["c"]), inner // len(number["u"]), width // 3
@@ -910,8 +918,8 @@
     )
     step = done[0]
 
-    def attention(qkv, lse, tokens_t, wq, dq, prep, turned, acc):
-        context = norm
+    def attention(qkv, tokens_t, wq, dq, prep, turned, acc):
+        context, lse = norm, scale
         block = min(256, length) if grid.with_fsdp else min(128, length)
         blocks = length // block
 
@@ -920,26 +928,54 @@
 
         for i in number["q"]:
             scatter.pieces[i] = (dq,) + scatter.pieces[i][1:]
-        loads = [copy(8, h_qkv, qkv), copy(9, h_context, context), copy(10, h_lse, lse), copy(11, h_tokens, tokens_t), copy(12, h_wq.at[:, 0:width], wp), copy(6, h_wq.at[:, width : 2 * width], wq.at[0]), copy(7, h_wq.at[:, 2 * width :], wq.at[1])]
+        span = width // groups
+
+        def group_loads(g):
+            for j in range(3):
+                cols = pl.ds(j * width + g * span, span)
+                yield pltpu.make_async_copy(h_qkv.at[:, cols], qkv.at[:, cols], pair_sems.at[j, g % 2])
+
+        for g in range(min(2, groups)):
+            for c in group_loads(g):
+                c.start()
+        loads = [copy(11, h_tokens, tokens_t), copy(12, h_wq.at[:, 0:width], wp)]
+        loads += [copy(6, h_wq.at[:, width : 2 * width], wq.at[0]), copy(7, h_wq.at[:, 2 * width :], wq.at[1])]
         for c in loads:
             c.start()
-        for c in loads[:3]:
+        for c in (copy(9, h_context, norm), copy(10, h_lse, scale)):
             c.wait()
-        groups = len(number["q"]) // 3
-        span = width // groups
         each = span // LANES * blocks
         slots = groups * each
         live = len_ref[0]
         head = [slice(h * HEAD_DIM, (h + 1) * HEAD_DIM) for h in range(2)]
-        marks = []
-        for g in range(groups):
-            lo, hi = (step if g == 0 else number["q"][3 * g - 3]), number["q"][3 * g]
-            marks += [(lo + j * (hi - lo) // each, lo + (j + 1) * (hi - lo) // each) for j in range(each)]
+        due, late = [[] for _ in range(slots)], []
+        for j, events in enumerate(steps[step:]):
+            due[j * (slots - each // 2) // (len(steps) - step)] += events
+        for g in range(groups - 1):
+            for stage in range(stages):
+                at, events = each * (g + 1) - 1 + SPACING * (stage + 1), [(i, stage) for i in number["q"][3 * g : 3 * g + 3]]
+                if at < slots:
+                    due[at] += events
+                else:
+                    late.append(events)
+        tail = [late[j] if j < len(late) else [] for j in range(max(stages, len(late)))]
+        for stage in range(stages):
+            tail[len(tail) - stages + stage] += [(i, stage) for i in number["q"][-3:] + [last]]
 
         def slot(t, _):
             pair, b = t // blocks, t % blocks
             rows = rows_of(b)
             one = pl.ds(pl.multiple_of(pair * LANES, LANES), LANES)
+
+            for g in range(groups):
+
+                @pl.when(t == g * each)
+                def _():
+                    for c in group_loads(g):
+                        c.wait()
+                    if g + 2 < groups:
+                        for c in group_loads(g + 2):
+                            c.start()
 
             @pl.when(b == 0)
             def _():
@@ -962,15 +998,15 @@
                 qkv[:, pl.ds(pl.multiple_of(2 * width + pair * LANES, LANES), LANES)] = acc[0].astype(bf16).T
 
             for k in range(slots):
-                if marks[k][1] > marks[k][0]:
+                if due[k]:
 
                     @pl.when(t == k)
                     def _():
-                        scatter.run(*marks[k])
+                        scatter.run(due[k])
 
             @pl.when(t == each - 1)
             def _():
-                loads[3].wait()
+                loads[0].wait()
 
             @pl.when(t % each == each - 1)
             def _():
@@ -997,18 +1033,16 @@
             folded = fold_vector(vec[j : j + 1, : grid.count * n], grid.count, n, pad)
             dsmall[:, :, :, :, j, :] = folded.reshape(grid.shape + (pad,))
         scatter.begin(number["s"][0])
-        at_step = number["q"][-3]
-        for c in loads[4:]:
+        for c in loads[1:]:
             c.wait()
-        rest, parts = scatter.steps - at_step, 4
-        rows = length // parts
-        for i in range(parts):
-            scatter.run(at_step + i * rest // parts, at_step + (i + 1) * rest // parts)
+        rows = length // len(tail)
+        for i, events in enumerate(tail):
             here = slice(i * rows, (i + 1) * rows)
             total = grad[here, :] + dotg(qkv[here, :width], wp[...], 1, 1)
             for j in range(2):
                 total = total + dotg(qkv[here, (j + 1) * width : (j + 2) * width], wq[j], 1, 1)
             low[here, :] = total.astype(bf16)
+            scatter.run(events)
         out = copy(13, low, h_tokens_grad)
         out.start()
         scatter.finish()
@@ -1018,7 +1052,6 @@
     pl.run_scoped(
         attention,
         pltpu.VMEM((length, 3 * width), bf16),
-        pltpu.VMEM((length, LANES), f32),
         pltpu.VMEM((width, length), bf16),
         pltpu.VMEM((2, width, width), bf16),
         pltpu.VMEM(grid.shape + (width // grid.count, 3 * width), bf16),
@@ -1076,7 +1109,41 @@
             collective_id=1, has_side_effects=True, vmem_limit_bytes=VMEM_LIMIT
         ),
         name="backward",
-    )(length_of, partners.reshape(-1, 1), firsts, *gains, *hbm)
+    )(length_of, partners.reshape(1, -1), firsts, *gains, *hbm)
+
+
+def finish_kernel(count, *refs):
+    wide, narrow, refs = refs[:count], refs[count : count + 3], refs[count + 3 :]
+    wide_out, refs = refs[:count], refs[count:]
+    vectors, (bias, loss), refs = refs[:-count - 4], refs[-count - 4 : -count - 2], refs[-count - 2 :]
+    bufs, (in_sem, out_sem) = refs[:count], refs[count:]
+    loads = [pltpu.make_async_copy(a, b, in_sem.at[i]) for i, (a, b) in enumerate(zip(wide, bufs))]
+    stores = [pltpu.make_async_copy(b, a, out_sem.at[i]) for i, (a, b) in enumerate(zip(wide_out, bufs))]
+    for c in loads:
+        c.start()
+    for j, ref in enumerate(vectors):
+        ref[...] = narrow[0][j : j + 1, : ref.shape[1]]
+    bias[...] = narrow[1][0:1, : bias.shape[1]]
+    loss[...] = narrow[2][0:1, 0:1]
+    for load, store in zip(loads, stores):
+        load.wait()
+        store.start()
+    for c in stores:
+        c.wait()
+
+
+def finish(wide, narrow, sizes):
+    vmem, anywhere = pl.BlockSpec(memory_space=pltpu.VMEM), pl.BlockSpec(memory_space=pl.ANY)
+    shape, count = jax.ShapeDtypeStruct, len(wide)
+    outs = pl.pallas_call(
+        functools.partial(finish_kernel, count),
+        out_shape=[shape(w.shape, w.dtype) for w in wide] + [shape((1, n), f32) for n in sizes] + [shape((1, 1), f32)],
+        in_specs=[anywhere] * count + [vmem] * 3,
+        out_specs=[anywhere] * count + [vmem] * (len(sizes) + 1),
+        scratch_shapes=[pltpu.VMEM(w.shape, w.dtype) for w in wide] + [pltpu.SemaphoreType.DMA((count,))] * 2,
+        name="results",
+    )(*wide, *narrow)
+    return outs[:count], [v.reshape(-1) for v in outs[count:-1]], outs[-1].reshape(())
 
 
 def on_device(whole, grid, tokens, lengths, keep_attn, keep_ffn, partners, out_cot, *weights):
@@ -1104,13 +1171,17 @@
     rq, ro, ru, rd, rs, pool_w, pool_b, loss, tokens_grad = run_backward(
         grid, whole, lengths, partners, firsts, [vectors[2], vectors[6]], hbm, length, width, inner, sizes, shard_rows
     )
-    owned = [rq, ro, ru, rd] + [rs[j, :n] for j, n in enumerate(sizes)]
-    if not grid.with_fsdp:
-        owned = [lax.psum_scatter(g, "fsdp", scatter_dimension=0, tiled=True) for g in owned]
-    rq, ro, ru, rd, s_qv, s_out, s_g1, s_b1, s_up, s_down, s_g2, s_b2 = owned
+    if grid.with_fsdp:
+        wide, vectors, loss = finish([layer_out, tokens_grad, rq, ro, ru, rd, pool_w], [rs, pool_b, loss], sizes + [shard_rows])
+        layer_out, tokens_grad, rq, ro, ru, rd, pool_w = wide
+    else:
+        owned = [rq, ro, ru, rd] + [rs[j, :n] for j, n in enumerate(sizes)]
+        rq, ro, ru, rd, *vectors = [lax.psum_scatter(g, "fsdp", scatter_dimension=0, tiled=True) for g in owned]
+        vectors, loss = vectors + [pool_b[0, :shard_rows]], loss[0, 0]
+    s_qv, s_out, s_g1, s_b1, s_up, s_down, s_g2, s_b2, s_pool = vectors
     return (
         layer_out.reshape(tokens.shape), tokens_grad.reshape(tokens.shape), rq, s_qv, ro, s_out, s_g1, s_b1, ru, s_up,
-        rd, s_down, s_g2, s_b2, pool_w, pool_b[0, :shard_rows], loss[0, 0],
+        rd, s_down, s_g2, s_b2, pool_w, s_pool, loss,
     )
 
 

time: 258 us -> 233 us (0.903)
  local copies, waits for them, and re-layouts: 13.6 us -> 0 us
  Pallas kernels: 243 us -> 232 us
    pallas_call x1, Pallas kernels: 144 us -> 128 us  [run_backward(): pl.pallas_call(functools.partial(backward_kernel, grid, whole, plan, size...]
    unnamed x19 -> x0, local copies, waits for them, and re-layouts: 7.32 us -> none
    pallas_call x0 -> x1, Pallas kernels: none -> 4.77 us  [finish(): pl.pallas_call(functools.partial(finish_kernel, count), out_shape=[shape(...]
    squeeze x3 -> x0, local copies, waits for them, and re-layouts: 3.8 us -> none  [on_device(): owned = [rq, ro, ru, rd] + [rs[j, :n] for j, n in enumerate(sizes)]]
where the time goes in v1:
time: 233 us
  Pallas kernels  232 us (100%)
    pallas_call x1, Pallas kernels, run_backward(): pl.pallas_call(functools.partial(backward_kernel, grid, whole, plan, size...  128 us
    pallas_call x1, Pallas kernels, run_forward(): pl.pallas_call(functools.partial(forward_kernel, grid, plan, sizes), out_...  99.2 us
    pallas_call x1, Pallas kernels, finish(): pl.pallas_call(functools.partial(finish_kernel, count), out_shape=[shape(...  4.77 us

profile of v1, /device:TPU:0, one launch (start us, length us, event | category | flops | bytes accessed | tf_op | source)
XLA Modules:
  0.0 233.1 jit_solution(5624330474225063917)
XLA Ops:
  1.3 99.2 %forward.1 = (bf16[4,2,2,2,24,2304]{5,4,3,2,1,0:T(8,128)(2,1)}, bf16[4,2,2,2,24,768]{5,4,3,2,1,0:T(8,128)(2,1)}, bf16[4,2,2,2,24,3072]{5,4,3,2,1,0:T(8,128)(2,1)...) custom-call(s32[1]{0:T(128)S(6)} %copy.37.refs_0_, ...), custom_call_target="tpu_custom_call" | custom-call | tf_op jit(solution)/shard_map/forward/pallas_call | solution.py:582
  100.5 127.6 %backward.1 = (f32[24,2304]{1,0:T(8,128)}, f32[24,768]{1,0:T(8,128)}, f32[24,3072]{1,0:T(8,128)}, f32[96,768]{1,0:T(8,128)}, f32[16,128]{1,0:T(8,128)}, /*index=...) custom-call(s32[1]{0:T(128)S(6)} %copy.37.refs_0_, s32[1,32]{1,0:T(1,128)} %bitcast.51, ...), custom_call_target="tpu_custom_call" | custom-call | tf_op jit(solution)/shard_map/backward/pallas_call | solution.py:1075
  228.1 4.8 %results.1 = (bf16[1024,768]{1,0:T(8,128)(2,1)}, bf16[1024,768]{1,0:T(8,128)(2,1)}, f32[24,2304]{1,0:T(8,128)}, f32[24,768]{1,0:T(8,128)}, f32[24,3072]{1,0:T(8,...) custom-call(bf16[1024,768]{1,0:T(8,128)(2,1)} %get-tuple-element.64., ...), custom_call_target="tpu_custom_call" | custom-call | tf_op jit(solution)/shard_map/results/pallas_call | solution.py:1138

commit v2 on v1

--- a/solution.py
+++ b/solution.py
@@ -20,14 +20,8 @@
 VMEM_LIMIT = 67043328
 DIMS = ("z", "c", "y", "x")
 SPACING = 4
-GATHER_ORDERS = (
-    ("z", "x", "y", "c"),
-    ("x", "z", "y", "c"),
-    ("z", "y", "x", "c"),
-    ("z", "y", "x", "c"),
-    ("y", "z", "x", "c"),
-    ("z", "x", "y", "c"),
-)
+SHARES = (0.56, 0.64, 0.88)
+GATHER_ORDERS = (("z", "x", "y", "c"), ("z", "y", "x", "c"))
 SCATTER_ORDERS = (("c", "y", "x", "z"), ("c", "x", "y", "z"))
 
 
@@ -252,7 +246,11 @@
         for copy in self.copies(i, stage):
             copy.wait_recv()
         buf = bufs[stage]
-        total = self.pick(i, stage, self.at[order[stage]])[...].astype(f32)
+        own = self.pick(i, stage, self.at[order[stage]])[...]
+        if stage < self.stages - 1 and self.grid.size[order[stage]] == 2:
+            buf[0] = own + buf[0]
+            return
+        total = own.astype(f32)
         for j in range(self.grid.size[order[stage]] - 1):
             total = total + buf[j].astype(f32)
         if stage == self.stages - 1:
@@ -448,10 +446,14 @@
         attend(qkv_ref, context, lse, prep, t // blocks, rows, block)
 
     slots = groups * each
-    first, last = end["q"][2], end["u"][len(end["u"]) // 2]
+    first, total = end["q"][2], len(gather.events)
+
+    def by_then(share):
+        return first + int(share * (total - first))
+
     gather.loop(
         slots,
-        [max(end["q"][3 * (t // each) + 2], first + t * (last - first) // slots) for t in range(slots)],
+        [max(end["q"][3 * (t // each) + 2], by_then(SHARES[0] * t / slots)) for t in range(slots)],
         attention,
     )
     put(gq, qkv_ref, context, lse)
@@ -478,7 +480,7 @@
         norm1[here, :] = norm.astype(bf16)
         scale1[here, :] = jnp.broadcast_to(scale, (block, LANES))
 
-    gather.loop(blocks, [gather.now] * blocks, project)
+    gather.loop(blocks, [by_then(SHARES[0] + (SHARES[1] - SHARES[0]) * t / blocks) for t in range(blocks)], project)
     load = pltpu.make_async_copy(keep_f, keep, keep_sem)
     load.start()
     put(go, hidden_t, context_t, norm1, scale1)
@@ -511,7 +513,7 @@
         for copy in saved(t, cols):
             copy.start()
 
-    gather.loop(parts, end["u"], up)
+    gather.loop(parts, [max(end["u"][t], by_then(SHARES[1] + (SHARES[2] - SHARES[1]) * t / parts)) for t in range(parts)], up)
     for t in range(max(0, parts - 2), parts):
         for copy in saved(t, pl.ds(0, step)):
             copy.wait()
@@ -766,9 +768,15 @@
         return 0
 
     held = -(-math.prod(whole.shape) // strip)
-    lax.fori_loop(held, strips, lambda t, _: second_norm(t, None), 0)
-    exchange.wait(0)
-    exchange.start(1)
+    def rest_of_norm(t, _):
+        @pl.when(t == (held + strips) // 2)
+        def _():
+            exchange.wait(0)
+            exchange.start(1)
+
+        return second_norm(t, None)
+
+    lax.fori_loop(held, strips, rest_of_norm, 0)
     exchange.wait(1)
     here = lax.axis_index("dp") * (whole.size["y"] * whole.size["x"]) + lax.axis_index("fsdp")
     pool_and_loss(views, partners_ref, wp[...], here, shard_rows, grad, gctx, cls_grad, pool_w, pool_b, loss)

time: 233 us -> 229 us (0.983)
  Pallas kernels: 232 us -> 227 us
    pallas_call x1, Pallas kernels: 99.2 us -> 96.4 us  [run_forward(): pl.pallas_call(functools.partial(forward_kernel, grid, plan, sizes), out_...]
where the time goes in v2:
time: 229 us; the launch traced here: 228 us
  Pallas kernels  227 us (99%)
    pallas_call x1, Pallas kernels, run_backward(): pl.pallas_call(functools.partial(backward_kernel, grid, whole, plan, size...  126 us
    pallas_call x1, Pallas kernels, run_forward(): pl.pallas_call(functools.partial(forward_kernel, grid, plan, sizes), out_...  96.4 us
    pallas_call x1, Pallas kernels, finish(): pl.pallas_call(functools.partial(finish_kernel, count), out_shape=[shape(...  4.77 us

profile of v2, /device:TPU:0, one launch (start us, length us, event | category | flops | bytes accessed | tf_op | source)
XLA Modules:
  0.0 228.3 jit_solution(13963724758588492641)
XLA Ops:
  1.3 96.4 %forward.1 = (bf16[4,2,2,2,24,2304]{5,4,3,2,1,0:T(8,128)(2,1)}, bf16[4,2,2,2,24,768]{5,4,3,2,1,0:T(8,128)(2,1)}, bf16[4,2,2,2,24,3072]{5,4,3,2,1,0:T(8,128)(2,1)...) custom-call(s32[1]{0:T(128)S(6)} %copy.37.refs_0_, ...), custom_call_target="tpu_custom_call" | custom-call | tf_op jit(solution)/shard_map/forward/pallas_call | solution.py:584
  97.7 125.6 %backward.1 = (f32[24,2304]{1,0:T(8,128)}, f32[24,768]{1,0:T(8,128)}, f32[24,3072]{1,0:T(8,128)}, f32[96,768]{1,0:T(8,128)}, f32[16,128]{1,0:T(8,128)}, /*index=...) custom-call(s32[1]{0:T(128)S(6)} %copy.37.refs_0_, s32[1,32]{1,0:T(1,128)} %bitcast.51, ...), custom_call_target="tpu_custom_call" | custom-call | tf_op jit(solution)/shard_map/backward/pallas_call | solution.py:1083
  223.3 4.8 %results.1 = (bf16[1024,768]{1,0:T(8,128)(2,1)}, bf16[1024,768]{1,0:T(8,128)(2,1)}, f32[24,2304]{1,0:T(8,128)}, f32[24,768]{1,0:T(8,128)}, f32[24,3072]{1,0:T(8,...) custom-call(bf16[1024,768]{1,0:T(8,128)(2,1)} %get-tuple-element.64., ...), custom_call_target="tpu_custom_call" | custom-call | tf_op jit(solution)/shard_map/results/pallas_call | solution.py:1146

commit v3 on v2

--- a/solution.py
+++ b/solution.py
@@ -373,15 +373,15 @@
 
 
 def forward_kernel(grid, plan, sizes, *refs):
-    (len_ref, tokens_ref, keep_a, keep_f, wq, wo, wu, wd, wp), refs = refs[:9], refs[9:]
+    (len_ref, h_tokens, keep_a, keep_f, wq, wo, wu, wd, wp), refs = refs[:9], refs[9:]
     count = len(sizes)
     small_in, refs = refs[:count], refs[count:]
     kept_hbm, (act_t, slope), refs = refs[:16], refs[16:18], refs[18:]
     firsts, small_out, refs = refs[0], refs[1 : 1 + count], refs[1 + count :]
     kept, refs = refs[:16], refs[16:]
     (gq, go, gu, gd, gp, qkv_ref, context, lse, tokens_t, context_t, hidden_t, norm1, scale1, norm2, scale2, layer_out) = kept
-    (gs, keep, hidden, hidden_low, act, act_buf, slope_buf, prep, bias), refs = refs[:9], refs[9:]
-    send, recv, own_sem, keep_sem, act_sem, slope_sem, out_sem = refs
+    (gs, tokens_ref, keep, hidden, hidden_low, act, act_buf, slope_buf, prep, bias), refs = refs[:10], refs[10:]
+    send, recv, own_sem, keep_sem, act_sem, slope_sem, out_sem, norm_sem = refs
     length, width = context.shape
     b_qv, b_out, g1, b1, b_up, b_down, g2, b2, b_pool = small_out
     outs = [pltpu.make_async_copy(src, dst, out_sem.at[i]) for i, (src, dst) in enumerate(zip(kept, kept_hbm))]
@@ -393,12 +393,12 @@
 
     at = grid.me()
     own = tuple(at[d] for d in DIMS)
-    load = pltpu.make_async_copy(keep_a, keep, keep_sem)
-    load.start()
     to_own = []
     for i, (src, dst) in enumerate(((wq, gq), (wo, go), (wu, gu), (wd, gd), (wp, gp))):
         to_own.append(pltpu.make_async_copy(src, dst.at[own], own_sem.at[i]))
         to_own[-1].start()
+    to_tokens = pltpu.make_async_copy(h_tokens, tokens_ref, own_sem.at[5])
+    to_tokens.start()
     mine = gs.at[own]
     mine[...] = jnp.zeros(mine.shape, bf16)
     for i, (ref, n) in enumerate(zip(small_in, sizes)):
@@ -413,6 +413,9 @@
     for copy in to_own:
         copy.wait()
     gather.begin()
+    load = pltpu.make_async_copy(keep_a, keep, keep_sem)
+    load.start()
+    to_tokens.wait()
     tokens_t[...] = tokens_ref[...].T
     lse[...] = jnp.zeros_like(lse)
     put(tokens_t)
@@ -535,6 +538,10 @@
     block = min(256, length)
     blocks = length // block
 
+    def left(t):
+        for j, i in enumerate((13, 14, 15)):
+            yield pltpu.make_async_copy(kept[i].at[row_block(t)], kept_hbm[i].at[row_block(t)], norm_sem.at[j, t])
+
     def norm(t):
         here = row_block(t)
         value, scale = normalize(hidden[here, :])
@@ -542,6 +549,8 @@
         norm2[here, :] = value.astype(bf16)
         scale2[here, :] = jnp.broadcast_to(scale, (block, LANES))
         layer_out[here, :] = out.astype(bf16)
+        for c in left(t):
+            c.start()
 
         @pl.when(t == 0)
         def _():
@@ -551,10 +560,12 @@
             firsts[1:2, :] = first[0:1].astype(f32)
 
     gather.loop(blocks, [gather.now] * blocks, norm)
-    put(norm2, scale2, layer_out)
     gather.finish()
-    for copy in outs:
+    for copy in outs[:13]:
         copy.wait()
+    for t in range(blocks):
+        for c in left(t):
+            c.wait()
 
 
 def run_forward(grid, length_of, tokens, keep_a, keep_f, big, small):
@@ -586,11 +597,12 @@
         out_shape=[shape(*k) for k in kept]
         + [shape((inner, length), bf16), shape((length, inner), bf16), shape((2, width), f32)]
         + [shape((1, grid.count * n), f32) for n in sizes],
-        in_specs=[pl.BlockSpec(memory_space=pltpu.SMEM), vmem, anywhere, anywhere] + [vmem] * (5 + len(small)),
+        in_specs=[pl.BlockSpec(memory_space=pltpu.SMEM)] + [anywhere] * 8 + [vmem] * len(small),
         out_specs=[anywhere] * 18 + [vmem] * (1 + len(small)),
         scratch_shapes=[pltpu.VMEM(*k) for k in kept]
         + [
             pltpu.VMEM(grid.shape + (16, pad), bf16),
+            pltpu.VMEM((length, width), bf16),
             pltpu.VMEM((length, width), jnp.int32),
             pltpu.VMEM((length, width), f32),
             pltpu.VMEM((length, width), bf16),
@@ -601,11 +613,12 @@
             pltpu.VMEM((1, 3 * width), f32),
             pltpu.SemaphoreType.DMA((len(plan), grid.slots)),
             pltpu.SemaphoreType.DMA((len(plan), grid.slots)),
-            pltpu.SemaphoreType.DMA((5,)),
+            pltpu.SemaphoreType.DMA((6,)),
             pltpu.SemaphoreType.DMA,
             pltpu.SemaphoreType.DMA((2,)),
             pltpu.SemaphoreType.DMA((2,)),
             pltpu.SemaphoreType.DMA((16,)),
+            pltpu.SemaphoreType.DMA((3, length // min(256, length))),
         ],
         compiler_params=pltpu.CompilerParams(
             collective_id=0, has_side_effects=True, vmem_limit_bytes=VMEM_LIMIT

time: 229 us -> 226 us (0.987)
  Pallas kernels: 227 us -> 224 us
where the time goes in v3:
time: 226 us
  Pallas kernels  224 us (99%)
    pallas_call x1, Pallas kernels, run_backward(): pl.pallas_call(functools.partial(backward_kernel, grid, whole, plan, size...  125 us
    pallas_call x1, Pallas kernels, run_forward(): pl.pallas_call(functools.partial(forward_kernel, grid, plan, sizes), out_...  94.3 us
    pallas_call x1, Pallas kernels, finish(): pl.pallas_call(functools.partial(finish_kernel, count), out_shape=[shape(...  4.77 us

profile of v3, /device:TPU:0, one launch (start us, length us, event | category | flops | bytes accessed | tf_op | source)
XLA Modules:
  0.0 226.0 jit_solution(9208526995752225823)
XLA Ops:
  1.3 94.3 %forward.1 = (bf16[4,2,2,2,24,2304]{5,4,3,2,1,0:T(8,128)(2,1)}, bf16[4,2,2,2,24,768]{5,4,3,2,1,0:T(8,128)(2,1)}, bf16[4,2,2,2,24,3072]{5,4,3,2,1,0:T(8,128)(2,1)...) custom-call(s32[1]{0:T(128)S(6)} %copy.37.refs_0_, ...), custom_call_target="tpu_custom_call" | custom-call | tf_op jit(solution)/shard_map/forward/pallas_call | solution.py:595
  95.6 125.4 %backward.1 = (f32[24,2304]{1,0:T(8,128)}, f32[24,768]{1,0:T(8,128)}, f32[24,3072]{1,0:T(8,128)}, f32[96,768]{1,0:T(8,128)}, f32[16,128]{1,0:T(8,128)}, /*index=...) custom-call(s32[1]{0:T(128)S(6)} %copy.37.refs_0_, s32[1,32]{1,0:T(1,128)} %bitcast.51, ...), custom_call_target="tpu_custom_call" | custom-call | tf_op jit(solution)/shard_map/backward/pallas_call | solution.py:1096
  221.0 4.8 %results.1 = (bf16[1024,768]{1,0:T(8,128)(2,1)}, bf16[1024,768]{1,0:T(8,128)(2,1)}, f32[24,2304]{1,0:T(8,128)}, f32[24,768]{1,0:T(8,128)}, f32[24,3072]{1,0:T(8,...) custom-call(bf16[1024,768]{1,0:T(8,128)(2,1)} %get-tuple-element.64., ...), custom_call_target="tpu_custom_call" | custom-call | tf_op jit(solution)/shard_map/results/pallas_call | solution.py:1159

commit v4 on v3

--- a/solution.py
+++ b/solution.py
@@ -20,7 +20,7 @@
 VMEM_LIMIT = 67043328
 DIMS = ("z", "c", "y", "x")
 SPACING = 4
-SHARES = (0.56, 0.64, 0.88)
+SHARES = (0.62, 0.68, 0.92)
 GATHER_ORDERS = (("z", "x", "y", "c"), ("z", "y", "x", "c"))
 SCATTER_ORDERS = (("c", "y", "x", "z"), ("c", "x", "y", "z"))
 

time: 226 us -> 225 us (level)
  no operation moved by 1% of the time
where the time goes in v4:
time: 225 us
  Pallas kernels  223 us (99%)
    pallas_call x1, Pallas kernels, run_backward(): pl.pallas_call(functools.partial(backward_kernel, grid, whole, plan, size...  126 us
    pallas_call x1, Pallas kernels, run_forward(): pl.pallas_call(functools.partial(forward_kernel, grid, plan, sizes), out_...  92.7 us
    pallas_call x1, Pallas kernels, finish(): pl.pallas_call(functools.partial(finish_kernel, count), out_shape=[shape(...  4.77 us

profile of v4, /device:TPU:0, one launch (start us, length us, event | category | flops | bytes accessed | tf_op | source)
XLA Modules:
  0.0 224.7 jit_solution(15535593598171548092)
XLA Ops:
  1.3 92.7 %forward.1 = (bf16[4,2,2,2,24,2304]{5,4,3,2,1,0:T(8,128)(2,1)}, bf16[4,2,2,2,24,768]{5,4,3,2,1,0:T(8,128)(2,1)}, bf16[4,2,2,2,24,3072]{5,4,3,2,1,0:T(8,128)(2,1)...) custom-call(s32[1]{0:T(128)S(6)} %copy.37.refs_0_, ...), custom_call_target="tpu_custom_call" | custom-call | tf_op jit(solution)/shard_map/forward/pallas_call | solution.py:595
  94.0 125.8 %backward.1 = (f32[24,2304]{1,0:T(8,128)}, f32[24,768]{1,0:T(8,128)}, f32[24,3072]{1,0:T(8,128)}, f32[96,768]{1,0:T(8,128)}, f32[16,128]{1,0:T(8,128)}, /*index=...) custom-call(s32[1]{0:T(128)S(6)} %copy.37.refs_0_, s32[1,32]{1,0:T(1,128)} %bitcast.51, ...), custom_call_target="tpu_custom_call" | custom-call | tf_op jit(solution)/shard_map/backward/pallas_call | solution.py:1096
  219.8 4.8 %results.1 = (bf16[1024,768]{1,0:T(8,128)(2,1)}, bf16[1024,768]{1,0:T(8,128)(2,1)}, f32[24,2304]{1,0:T(8,128)}, f32[24,768]{1,0:T(8,128)}, f32[24,3072]{1,0:T(8,...) custom-call(bf16[1024,768]{1,0:T(8,128)(2,1)} %get-tuple-element.64., ...), custom_call_target="tpu_custom_call" | custom-call | tf_op jit(solution)/shard_map/results/pallas_call | solution.py:1159
